TPU v7x, 256 devices: a whole 4x4x8 slice. The times are simulated.
256 devices in a mesh: copy: 4 (over x_hi, core), space: 64 (over y, z, x_lo).
Axes of the slice: x: 4 (x_hi: 2, x_lo: 2; x = x_hi * 2 + x_lo), y: 4, z: 8, core: 2. Of those that a mesh axis runs over, the one named last changes fastest.
Arguments:
- noisy_tokens: bfloat16 [4, 256, 256, 384], P('copy', 'space'), may hold values from -6 to 6
- grad_out: bfloat16 [4, 256, 256, 384], P('copy', 'space'), may hold values from -6 to 6
- filter_weight: bfloat16 [2, 256, 256, 384], P(None, None, 'space'), may hold values from -4 to 4
- weight_in: bfloat16 [384, 1536], replicated, may hold values from -0.3125 to 0.3125
- weight_out: bfloat16 [1536, 384], replicated, may hold values from -0.15625 to 0.15625
- gain_one: float32 [384], replicated, may hold values from 0.1 to 1.9
- gain_two: float32 [384], replicated, may hold values from 0.1 to 1.9
Outputs:
- block_out: bfloat16 [4, 256, 256, 384], P('copy', 'space')
- grad_tokens: bfloat16 [4, 256, 256, 384], P('copy', 'space')
- grad_filter: float32 [2, 256, 256, 384], P(None, None, 'space')
- grad_weight_in: bfloat16 [384, 1536], replicated
- grad_weight_out: bfloat16 [1536, 384], replicated
- grad_gain_one: float32 [384], replicated
- grad_gain_two: float32 [384], replicated
All inputs are finite; a program needn't handle non-finite values.
Results may differ from a plain program's by a relative error of at most 0.024.
Values may be sent and summed in bfloat16 or wider, within the bound.
A program may use at most 128 MiB of HBM per device.

v0:
```python
import math
import jax
import jax.numpy as jnp
from jax import lax
from jax.sharding import PartitionSpec as P

EPS = 1e-06


def dft_parts(length):
    index = jnp.arange(length, dtype=jnp.int32)
    phase = index[:, None] * index[None, :] % length
    angle = phase.astype(jnp.float32) * (2.0 * math.pi / length)
    factor = 1.0 / math.sqrt(length)
    return (
        (jnp.cos(angle) * factor).astype(jnp.bfloat16),
        (jnp.sin(angle) * factor).astype(jnp.bfloat16),
    )


def row_table(length):
    cosine, sine = dft_parts(length)
    return jnp.stack([cosine, -sine])


def column_table(length, direction):
    cosine, sine = dft_parts(length)
    upper = jnp.stack([cosine, direction * sine], axis=1)
    lower = jnp.stack([-direction * sine, cosine], axis=1)
    return jnp.stack([upper, lower])


def layer_norm(values):
    centre = jnp.mean(values, axis=-1, keepdims=True)
    centred = values - centre
    variance = jnp.mean(centred * centred, axis=-1, keepdims=True)
    rstd_value = lax.rsqrt(variance + EPS)
    return (centred * rstd_value, rstd_value)


def norm_backward(upstream, normed, rstd_value, gain):
    scaled = upstream * gain
    result = (
        scaled
        - jnp.mean(scaled, axis=-1, keepdims=True)
        - normed * jnp.mean(scaled * normed, axis=-1, keepdims=True)
    ) * rstd_value
    lead = tuple(range(upstream.ndim - 1))
    return (result, jnp.sum(upstream * normed, axis=lead))


def apply_filter(spectrum, filter_weight, direction):
    real_part = spectrum[0].astype(jnp.float32)
    imag_part = spectrum[1].astype(jnp.float32)
    kernel_real = filter_weight[0].astype(jnp.float32)
    kernel_imag = direction * filter_weight[1].astype(jnp.float32)
    return jnp.stack(
        [
            kernel_real * real_part - kernel_imag * imag_part,
            kernel_real * imag_part + kernel_imag * real_part,
        ]
    )


def exact_gelu(values):
    return jax.nn.gelu(values, approximate=False)


def spectral(values, filter_weight, direction):
    width = values.shape[2]
    rows_tab = row_table(width)
    rows = jnp.einsum(
        "pkw,bhwc->pbhkc", rows_tab, values, preferred_element_type=jnp.float32
    ).astype(jnp.bfloat16)
    columns = lax.all_to_all(rows, "space", split_axis=3, concat_axis=2, tiled=True)
    height = columns.shape[2]
    spectrum = jnp.einsum(
        "qmph,pbhkc->qbmkc", column_table(height, 1), columns, preferred_element_type=jnp.float32
    ).astype(jnp.bfloat16)
    weighted = apply_filter(spectrum, filter_weight[:, None], direction).astype(jnp.bfloat16)
    returned = jnp.einsum(
        "qmph,pbhkc->qbmkc", column_table(height, -1), weighted, preferred_element_type=jnp.float32
    ).astype(jnp.bfloat16)
    back_rows = lax.all_to_all(returned, "space", split_axis=2, concat_axis=3, tiled=True)
    output = jnp.einsum("pkw,pbhkc->bhwc", rows_tab, back_rows, preferred_element_type=jnp.float32)
    return (output, spectrum)


def body(noisy_tokens, grad_out, filter_weight, weight_in, weight_out, gain_one, gain_two):
    batch, rows_dev, width, chans = noisy_tokens.shape
    inputs = noisy_tokens.astype(jnp.float32)
    normed_one, rstd_one = layer_norm(inputs)
    mixed_in = (normed_one * gain_one).astype(jnp.bfloat16)
    spatial, spectrum = spectral(mixed_in, filter_weight, 1)
    normed_two, rstd_two = layer_norm(spatial)
    mlp_in = (normed_two * gain_two).astype(jnp.bfloat16).reshape(-1, chans)
    preact = jnp.dot(mlp_in, weight_in, preferred_element_type=jnp.float32)
    activated = exact_gelu(preact).astype(jnp.bfloat16)
    mlp_out = jnp.dot(activated, weight_out, preferred_element_type=jnp.float32)
    block_out = (inputs + mlp_out.reshape(inputs.shape)).astype(jnp.bfloat16)
    upstream = grad_out.reshape(-1, chans)
    grad_act = jnp.dot(upstream, weight_out.T, preferred_element_type=jnp.float32)
    grad_pre = jax.vjp(exact_gelu, preact)[1](grad_act)[0].astype(jnp.bfloat16)
    sum_out = jnp.dot(activated.T, upstream, preferred_element_type=jnp.float32)
    sum_in = jnp.dot(mlp_in.T, grad_pre, preferred_element_type=jnp.float32)
    grad_mlp = jnp.dot(grad_pre, weight_in.T, preferred_element_type=jnp.float32).reshape(
        inputs.shape
    )
    grad_spatial, sum_gain_two = norm_backward(grad_mlp, normed_two, rstd_two, gain_two)
    back_spatial, adjoint = spectral(grad_spatial.astype(jnp.bfloat16), filter_weight, -1)
    spec_f = spectrum.astype(jnp.float32)
    adj_f = adjoint.astype(jnp.float32)
    filter_terms = jnp.stack(
        [
            jnp.sum(adj_f[0] * spec_f[0] + adj_f[1] * spec_f[1], axis=0),
            jnp.sum(adj_f[1] * spec_f[0] - adj_f[0] * spec_f[1], axis=0),
        ]
    )
    grad_filter = lax.psum(filter_terms.astype(jnp.bfloat16), "copy").astype(jnp.float32)
    grad_normed, sum_gain_one = norm_backward(back_spatial, normed_one, rstd_one, gain_one)
    grad_tokens = (grad_out.astype(jnp.float32) + grad_normed).astype(jnp.bfloat16)
    local_sums = (sum_in, sum_out, sum_gain_one, sum_gain_two)
    summed = lax.psum(
        (local_sums[0], local_sums[1], local_sums[2], local_sums[3]), ("copy", "space")
    )
    total_tokens = batch * lax.axis_size("copy") * rows_dev * lax.axis_size("space") * width
    factor = 1.0 / math.sqrt(total_tokens)
    return (
        block_out,
        grad_tokens,
        grad_filter,
        (summed[0] * factor).astype(jnp.bfloat16),
        (summed[1] * factor).astype(jnp.bfloat16),
        summed[2] * factor,
        summed[3] * factor,
    )


def solution(mesh):
    return jax.shard_map(
        body,
        mesh=mesh,
        in_specs=(
            P("copy", "space", None, None),
            P("copy", "space", None, None),
            P(None, None, "space", None),
            P(),
            P(),
            P(),
            P(),
        ),
        out_specs=(
            P("copy", "space", None, None),
            P("copy", "space", None, None),
            P(None, None, "space", None),
            P(),
            P(),
            P(),
            P(),
        ),
        check_vma=False,
    )
```

profile of v0, /device:TPU:1, one launch (start us, length us, event | category | flops | bytes accessed | tf_op | source)
XLA Modules:
  0.0 629.1 jit_solution(3767009619410764740)
XLA Ops:
  13.5 3.0 copy.69
  16.5 13.8 %all-to-all-start = ((bf16[2,1,4,256,384]{4,0,2,1,3:T(2,128)(2,1)}), bf16[2,1,4,256,384]{4,0,2,1,3:T(2,128)(2,1)}, u32[]{:S(2)}, u32[]{:S(2)}) async-start(bf16[2,1,4,256,384]{4,0,2,1,3:T(2,128)(2,1)} %copy.69), calls=%async_computation | async-start | bytes 3145728 | tf_op jit(solution)/shard_map/all_to_all | solution.py:75
  30.3 2.8 fusion.94
  38.8 29.9 %all-to-all-done = bf16[2,1,4,256,384]{4,0,2,1,3:T(2,128)(2,1)} async-done(((bf16[2,1,4,256,384]{4,0,2,1,3:T(2,128)(2,1)}), bf16[2,1,4,256,384]{4,0,2,1,3:T(2,128)(2,1)}, u32[]{:S(2)}, u32[]{:S(2)}) %all-to-all-start) | async-done | bytes 1572896 | tf_op jit(solution)/shard_map/all_to_all | solution.py:75
  71.7 2.7 fusion.95
  77.6 4.3 copy.77
  81.9 45.2 %all_to_all.60 = bf16[2,1,256,4,384]{4,0,3,1,2:T(2,128)(2,1)S(1)} all-to-all(bf16[2,1,256,4,384]{4,0,3,1,2:T(2,128)(2,1)S(1)} %copy.77), channel_id=1, replica_groups=mesh['copy'=4,'space'=64] {'space'}, dimensions={2} | all-to-all | bytes 3145728 | tf_op jit(solution)/shard_map/all_to_all | solution.py:84
  129.7 2.3 bitcast_reduce_fusion
  133.1 15.5 %multiply_convert_fusion = (bf16[1024,1536]{1,0:T(8,128)(2,1)}, f32[1024,1536]{1,0:T(8,128)S(1)}, f32[1024,1536]{1,0:T(8,128)S(1)}) fusion(bf16[1024,384]{1,0:T(8,128)(2,1)S(1)} %bitcast.255, bf16[384,1536]{1,0:T(8,128)(2,1)S(1)} %copy-done), kind=kOutput, calls=%fused_computation.3 | convolution fusion | flops 1310195712 | bytes 17694720 | tf_op jit(solution)/shard_map/dot_general | solution.py:97
  148.6 3.3 add_convert_fusion
  157.4 4.0 fusion.40
  161.3 4.9 copy.84
  166.2 7.7 %all-to-all-start.2 = ((bf16[2,1,4,256,384]{4,0,2,1,3:T(2,128)(2,1)}), bf16[2,1,4,256,384]{4,0,2,1,3:T(2,128)(2,1)S(1)}, u32[]{:S(2)}, u32[]{:S(2)}) async-start(bf16[2,1,4,256,384]{4,0,2,1,3:T(2,128)(2,1)} %copy.84), calls=%async_computation.2 | async-start | bytes 3145728 | tf_op jit(solution)/shard_map/all_to_all | solution.py:75
  174.2 5.2 fusion.98
  179.3 3.2 fusion.99
  182.6 31.1 %all-to-all-done.2 = bf16[2,1,4,256,384]{4,0,2,1,3:T(2,128)(2,1)S(1)} async-done(((bf16[2,1,4,256,384]{4,0,2,1,3:T(2,128)(2,1)}), bf16[2,1,4,256,384]{4,0,2,1,3:T(2,128)(2,1)S(1)}, u32[]{:S(2)}, u32[]{:S(2)}) %all-to-all-start.2) | async-done | bytes 1572896 | tf_op jit(solution)/shard_map/all_to_all | solution.py:75
  214.9 2.6 copy.87
  217.5 4.3 fusion.96
  223.9 3.1 copy.90
  227.0 8.3 %all-to-all-start.3 = ((bf16[2,1,256,4,384]{4,0,3,1,2:T(2,128)(2,1)}), bf16[2,1,256,4,384]{4,0,3,1,2:T(2,128)(2,1)S(1)}, u32[]{:S(2)}, u32[]{:S(2)}) async-start(bf16[2,1,256,4,384]{4,0,3,1,2:T(2,128)(2,1)} %copy.90), calls=%async_computation.3 | async-start | bytes 3145728 | tf_op jit(solution)/shard_map/all_to_all | solution.py:84
  235.6 3.4 fusion.57
  242.4 2.3 copy.82
  244.7 5.1 fusion.97
  249.8 3.1 copy.81
  252.9 215.0 %all-reduce.7.cloned.1.call-done = (f32[384,1536]{1,0:T(8,128)}, f32[1536,384]{1,0:T(8,128)}) async-done(((f32[384,1536]{1,0:T(8,128)}, f32[1536,384]{1,0:T(8,128)}), (f32[384,1536]{1,0:T(8,128)}, f32[1536,384]{1,0:T(8,128)})) %all-reduce.7.cloned.1.call-update) | async-done | bytes 4718608 | tf_op jit(solution)/shard_map/psum | solution.py:123
  467.9 3.0 multiply_convert_fusion.1
  472.0 55.6 %all-reduce.5.cloned.1.call-done = bf16[2,256,4,384]{1,3,2,0:T(8,128)(2,1)} async-done(((bf16[2,256,4,384]{1,3,2,0:T(8,128)(2,1)}), bf16[2,256,4,384]{1,3,2,0:T(8,128)(2,1)}) %all-reduce.5.cloned.1.call-update) | async-done | bytes 1572880 | tf_op jit(solution)/shard_map/psum | solution.py:119
  527.7 3.9 copy.100
  533.1 2.6 fusion.18
  535.7 76.1 %all-reduce = (f32[384]{0:T(512)}, f32[384]{0:T(512)}) all-reduce(f32[384]{0:T(512)} %get-tuple-element.28, f32[384]{0:T(512)S(1)} %copy-done.27), channel_id=1, replica_groups=mesh['copy'=4,'space'=64] {'copy','space'}, use_global_device_ids=true, to_apply=%region_12.13 | all-reduce | flops 768 | bytes 6144 | tf_op jit(solution)/shard_map/psum | solution.py:123
  615.1 3.4 fusion.17
  618.5 2.4 copy.98
  (114 shorter events, 41.3 us)
Async XLA Ops:
  7.2 125.9 %copy-start = (bf16[384,1536]{1,0:T(8,128)(2,1)S(1)}, bf16[384,1536]{1,0:T(8,128)(2,1)}, u32[]{:S(2)}) copy-start(bf16[384,1536]{1,0:T(8,128)(2,1)} %param.10) | copy-start | bytes 3538948
  10.5 1.8 copy-start.28
  11.9 1.0 copy-start.15
  12.8 3.7 copy-start.25
  16.5 52.1 %all-to-all-start = ((bf16[2,1,4,256,384]{4,0,2,1,3:T(2,128)(2,1)}), bf16[2,1,4,256,384]{4,0,2,1,3:T(2,128)(2,1)}, u32[]{:S(2)}, u32[]{:S(2)}) async-start(bf16[2,1,4,256,384]{4,0,2,1,3:T(2,128)(2,1)} %copy.69), calls=%async_computation | async-start | bytes 3145728 | tf_op jit(solution)/shard_map/all_to_all | solution.py:75
  33.8 40.6 %copy-start.4 = (bf16[1,256,4,384]{1,3,2,0:T(8,128)(2,1)}, bf16[1,256,4,384]{1,3,2,0:T(8,128)(2,1)S(1)}, u32[]{:S(2)}) copy-start(bf16[1,256,4,384]{1,3,2,0:T(8,128)(2,1)S(1)} %copy.124) | copy-start | bytes 2359300
  35.6 38.8 %copy-start.6 = (bf16[1,256,4,384]{1,3,2,0:T(8,128)(2,1)}, bf16[1,256,4,384]{1,3,2,0:T(8,128)(2,1)S(1)}, u32[]{:S(2)}) copy-start(bf16[1,256,4,384]{1,3,2,0:T(8,128)(2,1)S(1)} %copy.126) | copy-start | bytes 2359300
  70.6 1.0 copy-start.12
  74.4 1.0 copy-start.22
  133.0 15.5 %copy-start.19 = (bf16[1,4,256,384]{3,2,1,0:T(8,128)(2,1)}, bf16[1,4,256,384]{3,2,1,0:T(8,128)(2,1)S(1)}, u32[]{:S(2)}) copy-start(bf16[1,4,256,384]{3,2,1,0:T(8,128)(2,1)S(1)} %multiply_convert_fusion.4) | copy-start | bytes 2359300
  133.0 15.5 %copy-start.17 = (bf16[1,4,256,384]{3,2,1,0:T(8,128)(2,1)S(1)}, bf16[1,4,256,384]{3,2,1,0:T(8,128)(2,1)}, u32[]{:S(2)}) copy-start(bf16[1,4,256,384]{3,2,1,0:T(8,128)(2,1)} %param.8) | copy-start | bytes 2359300
  133.1 15.5 %copy-start.30 = (bf16[1536,384]{1,0:T(8,128)(2,1)S(1)}, bf16[1536,384]{1,0:T(8,128)(2,1)}, u32[]{:S(2)}) copy-start(bf16[1536,384]{1,0:T(8,128)(2,1)} %param.11) | copy-start | bytes 3538948
  151.8 1.9 copy-start.31
  153.8 1.2 copy-start.3
  166.2 47.4 %all-to-all-start.2 = ((bf16[2,1,4,256,384]{4,0,2,1,3:T(2,128)(2,1)}), bf16[2,1,4,256,384]{4,0,2,1,3:T(2,128)(2,1)S(1)}, u32[]{:S(2)}, u32[]{:S(2)}) async-start(bf16[2,1,4,256,384]{4,0,2,1,3:T(2,128)(2,1)} %copy.84), calls=%async_computation.2 | async-start | bytes 3145728 | tf_op jit(solution)/shard_map/all_to_all | solution.py:75
  173.9 293.9 %all-reduce.7.cloned.1.call-start = ((), (), s32[]{:S(2)}) async-start(), calls=%async_computation.5 | async-start | bytes 9437184 | tf_op jit(solution)/shard_map/psum | solution.py:123
  174.1 5.2 copy-start.18
  174.1 5.2 copy-start.32
  217.5 4.3 copy-start.5
  217.5 4.3 copy-start.7
  221.8 1.0 copy-start.21
  221.8 1.0 copy-start.23
  227.0 304.5 %all-to-all-start.3 = ((bf16[2,1,256,4,384]{4,0,3,1,2:T(2,128)(2,1)}), bf16[2,1,256,4,384]{4,0,3,1,2:T(2,128)(2,1)S(1)}, u32[]{:S(2)}, u32[]{:S(2)}) async-start(bf16[2,1,256,4,384]{4,0,3,1,2:T(2,128)(2,1)} %copy.90), calls=%async_computation.3 | async-start | bytes 3145728 | tf_op jit(solution)/shard_map/all_to_all | solution.py:84
  235.3 292.3 %all-reduce.5.cloned.1.call-start = ((), (), s32[]{:S(2)}) async-start(), calls=%async_computation.4 | async-start | bytes 3145728 | tf_op jit(solution)/shard_map/psum | solution.py:119
  235.6 3.9 copy-start.1
  235.6 4.8 copy-start.2
  467.8 3.0 copy-start.10
  532.2 1.0 copy-start.16
  532.2 1.0 copy-start.26
  533.1 2.6 copy-start.27
  533.1 81.9 %copy-start.8 = (f32[1,4,256,384]{2,3,1,0:T(8,128)S(1)}, f32[1,4,256,384]{2,3,1,0:T(8,128)}, u32[]{:S(2)}) copy-start(f32[1,4,256,384]{2,3,1,0:T(8,128)} %copy.81) | copy-start | bytes 4718596
  618.5 2.4 copy-start.9
  (6 other events, 5.3 us)
Sparse Core Ops, SparseCore 0:
  182.7 285.0 all-reduce.6
  470.7 56.9 all-reduce.4
where the time goes:
time: 639 us; the launch traced here: 629 us
  waiting for transfers between devices  332 us (52%)
  blocking collectives  121 us (19%)
  matrix products  53.9 us (8%)
  local copies, waits for them, and re-layouts  50 us (8%)
  starting transfers between devices  30.3 us (5%)
  other arithmetic  27.3 us (4%)
  between operations  14.7 us (2%)
    psum x1, waiting for transfers between devices, body(): lax.psum((local_sums[0], local_sums[1], local_sums[2], local_sums[3]), ('...  215 us
    psum x1, blocking collectives, body(): lax.psum((local_sums[0], local_sums[1], local_sums[2], local_sums[3]), ('...  76.1 us
    all_to_all x2, waiting for transfers between devices, spectral(): lax.all_to_all(rows, 'space', split_axis=3, concat_axis=2, tiled=True)  61 us
    psum x1, waiting for transfers between devices, body(): lax.psum(filter_terms.astype(jnp.bfloat16), 'copy').astype(jnp.float32)  55.6 us
    all_to_all x1, blocking collectives, spectral(): lax.all_to_all(returned, 'space', split_axis=2, concat_axis=3, tiled=True)  45.2 us
    all_to_all x2, starting transfers between devices, spectral(): lax.all_to_all(rows, 'space', split_axis=3, concat_axis=2, tiled=True)  21.5 us
    unnamed x73, local copies, waits for them, and re-layouts  17.3 us
    dot_general x1, matrix products, body(): preact = jnp.dot(mlp_in, weight_in, preferred_element_type=jnp.float32)  15.5 us
  transfers between devices with their start and end apart: 5, of which 4 were waited for; matrix products, arithmetic and copies ran while one was open for 9% of the time, Pallas kernels for 0%

commit v1 on v0

--- a/solution.py
+++ b/solution.py
@@ -1,3 +1,4 @@
+import functools
 import math
 import jax
 import jax.numpy as jnp
@@ -5,6 +6,15 @@
 from jax.sharding import PartitionSpec as P
 
 EPS = 1e-06
+
+
+def use_the_unit(matrix, which_axis):
+    piece_now = lax.all_gather(matrix, which_axis)
+    b_now = jnp.sum(piece_now, axis=0)
+    return b_now
+
+
+_derive_heads = functools.partial(use_the_unit, which_axis="copy")
 
 
 def dft_parts(length):
@@ -116,7 +126,7 @@
             jnp.sum(adj_f[1] * spec_f[0] - adj_f[0] * spec_f[1], axis=0),
         ]
     )
-    grad_filter = lax.psum(filter_terms.astype(jnp.bfloat16), "copy").astype(jnp.float32)
+    grad_filter = _derive_heads(filter_terms.astype(jnp.bfloat16)).astype(jnp.float32)
     grad_normed, sum_gain_one = norm_backward(back_spatial, normed_one, rstd_one, gain_one)
     grad_tokens = (grad_out.astype(jnp.float32) + grad_normed).astype(jnp.bfloat16)
     local_sums = (sum_in, sum_out, sum_gain_one, sum_gain_two)

time: 639 us -> 616 us (0.964)
  waiting for transfers between devices: 332 us -> 317 us
    psum x1 -> x0, waiting for transfers between devices: 55.6 us -> none  [body(): lax.psum(filter_terms.astype(jnp.bfloat16), 'copy').astype(jnp.float32)]
    psum x1, waiting for transfers between devices: 215 us -> 256 us  [body(): lax.psum((local_sums[0], local_sums[1], local_sums[2], local_sums[3]), ('...]
    unnamed x73 -> x75, local copies, waits for them, and re-layouts: 17.3 us -> 15.4 us
  transfers between devices with their start and end apart: 5 -> 5, of which waited for: 4 -> 3; matrix products, arithmetic and copies ran while one was open for 9% -> 8% of each run, Pallas kernels for 0% -> 0%
where the time goes in v1:
time: 616 us; the launch traced here: 607 us
  waiting for transfers between devices  317 us (51%)
  blocking collectives  123 us (20%)
  matrix products  50.2 us (8%)
  local copies, waits for them, and re-layouts  45.4 us (7%)
  starting transfers between devices  30.2 us (5%)
  other arithmetic  24.4 us (4%)
  between operations  16.2 us (3%)
    psum x1, waiting for transfers between devices, body(): lax.psum((local_sums[0], local_sums[1], local_sums[2], local_sums[3]), ('...  256 us
    psum x1, blocking collectives, body(): lax.psum((local_sums[0], local_sums[1], local_sums[2], local_sums[3]), ('...  77.8 us
    all_to_all x2, waiting for transfers between devices, spectral(): lax.all_to_all(rows, 'space', split_axis=3, concat_axis=2, tiled=True)  61.1 us
    all_to_all x1, blocking collectives, spectral(): lax.all_to_all(returned, 'space', split_axis=2, concat_axis=3, tiled=True)  45.2 us
    all_to_all x2, starting transfers between devices, spectral(): lax.all_to_all(rows, 'space', split_axis=3, concat_axis=2, tiled=True)  21.5 us
    dot_general x1, matrix products, body(): preact = jnp.dot(mlp_in, weight_in, preferred_element_type=jnp.float32)  15.5 us
    unnamed x75, local copies, waits for them, and re-layouts  15.4 us
  transfers between devices with their start and end apart: 5, of which 3 were waited for; matrix products, arithmetic and copies ran while one was open for 8% of the time, Pallas kernels for 0%

profile of v1, /device:TPU:1, one launch (start us, length us, event | category | flops | bytes accessed | tf_op | source)
XLA Modules:
  0.0 606.8 jit_solution(4714788871624768242)
XLA Ops:
  14.3 3.0 copy.59
  17.3 13.8 %all-to-all-start = ((bf16[2,1,4,256,384]{4,0,2,1,3:T(2,128)(2,1)}), bf16[2,1,4,256,384]{4,0,2,1,3:T(2,128)(2,1)}, u32[]{:S(2)}, u32[]{:S(2)}) async-start(bf16[2,1,4,256,384]{4,0,2,1,3:T(2,128)(2,1)} %copy.59), calls=%async_computation | async-start | bytes 3145728 | tf_op jit(solution)/shard_map/all_to_all | solution.py:85
  31.2 2.8 fusion.86
  34.6 1.8 copy.113
  39.6 29.9 %all-to-all-done = bf16[2,1,4,256,384]{4,0,2,1,3:T(2,128)(2,1)} async-done(((bf16[2,1,4,256,384]{4,0,2,1,3:T(2,128)(2,1)}), bf16[2,1,4,256,384]{4,0,2,1,3:T(2,128)(2,1)}, u32[]{:S(2)}, u32[]{:S(2)}) %all-to-all-start) | async-done | bytes 1572896 | tf_op jit(solution)/shard_map/all_to_all | solution.py:85
  69.5 2.0 copy.60
  72.5 2.7 fusion.87
  76.2 2.2 fusion.40
  78.4 4.3 copy.67
  82.8 45.2 %all_to_all.60 = bf16[2,1,256,4,384]{4,0,3,1,2:T(2,128)(2,1)S(1)} all-to-all(bf16[2,1,256,4,384]{4,0,3,1,2:T(2,128)(2,1)S(1)} %copy.67), channel_id=1, replica_groups=mesh['copy'=4,'space'=64] {'space'}, dimensions={2} | all-to-all | bytes 3145728 | tf_op jit(solution)/shard_map/all_to_all | solution.py:94
  130.5 2.3 bitcast_reduce_fusion
  133.9 15.5 %multiply_convert_fusion = (bf16[1024,1536]{1,0:T(8,128)(2,1)}, f32[1024,1536]{1,0:T(8,128)S(1)}, f32[1024,1536]{1,0:T(8,128)S(1)}) fusion(bf16[1024,384]{1,0:T(8,128)(2,1)S(1)} %bitcast.216, bf16[384,1536]{1,0:T(8,128)(2,1)S(1)} %copy-done), kind=kOutput, calls=%fused_computation.3 | convolution fusion | flops 1310195712 | bytes 17694720 | tf_op jit(solution)/shard_map/dot_general | solution.py:107
  149.4 3.3 add_convert_fusion
  152.7 1.9 multiply_reduce_fusion.2
  158.2 3.9 fusion.36
  162.1 5.0 copy.74
  167.1 7.6 %all-to-all-start.2 = ((bf16[2,1,4,256,384]{4,0,2,1,3:T(2,128)(2,1)}), bf16[2,1,4,256,384]{4,0,2,1,3:T(2,128)(2,1)S(1)}, u32[]{:S(2)}, u32[]{:S(2)}) async-start(bf16[2,1,4,256,384]{4,0,2,1,3:T(2,128)(2,1)} %copy.74), calls=%async_computation.2 | async-start | bytes 3145728 | tf_op jit(solution)/shard_map/all_to_all | solution.py:85
  175.0 5.1 fusion.90
  180.1 3.3 fusion.91
  183.4 31.2 %all-to-all-done.2 = bf16[2,1,4,256,384]{4,0,2,1,3:T(2,128)(2,1)S(1)} async-done(((bf16[2,1,4,256,384]{4,0,2,1,3:T(2,128)(2,1)}), bf16[2,1,4,256,384]{4,0,2,1,3:T(2,128)(2,1)S(1)}, u32[]{:S(2)}, u32[]{:S(2)}) %all-to-all-start.2) | async-done | bytes 1572896 | tf_op jit(solution)/shard_map/all_to_all | solution.py:85
  216.3 2.2 fusion.88
  221.7 2.1 fusion.21
  224.8 3.0 copy.80
  227.9 8.5 %all-to-all-start.3 = ((bf16[2,1,256,4,384]{4,0,3,1,2:T(2,128)(2,1)}), bf16[2,1,256,4,384]{4,0,3,1,2:T(2,128)(2,1)S(1)}, u32[]{:S(2)}, u32[]{:S(2)}) async-start(bf16[2,1,256,4,384]{4,0,3,1,2:T(2,128)(2,1)} %copy.80), calls=%async_computation.3 | async-start | bytes 3145728 | tf_op jit(solution)/shard_map/all_to_all | solution.py:94
  236.3 2.4 copy.72
  238.7 5.2 fusion.89
  244.0 3.0 copy.71
  247.0 256.4 %all-reduce.4.cloned.1.call-done = (f32[384,1536]{1,0:T(8,128)}, f32[1536,384]{1,0:T(8,128)}) async-done(((f32[384,1536]{1,0:T(8,128)}, f32[1536,384]{1,0:T(8,128)}), (f32[384,1536]{1,0:T(8,128)}, f32[1536,384]{1,0:T(8,128)})) %all-reduce.4.cloned.1.call-update) | async-done | bytes 4718608 | tf_op jit(solution)/shard_map/psum | solution.py:133
  503.3 3.0 multiply_convert_fusion.1
  513.8 77.8 %all-reduce = (f32[384]{0:T(512)S(1)}, f32[384]{0:T(512)S(1)}) all-reduce(f32[384]{0:T(512)S(1)} %get-tuple-element.28, f32[384]{0:T(512)S(1)} %copy-done.28), channel_id=1, replica_groups=mesh['copy'=4,'space'=64] {'copy','space'}, use_global_device_ids=true, to_apply=%region_12.13 | all-reduce | flops 768 | bytes 6144 | tf_op jit(solution)/shard_map/psum | solution.py:133
  592.8 3.9 reduce_sum.118
  596.7 2.4 copy.86
  (115 shorter events, 33.9 us)
Async XLA Ops:
  8.0 125.9 %copy-start = (bf16[384,1536]{1,0:T(8,128)(2,1)S(1)}, bf16[384,1536]{1,0:T(8,128)(2,1)}, u32[]{:S(2)}) copy-start(bf16[384,1536]{1,0:T(8,128)(2,1)} %param.10) | copy-start | bytes 3538948
  11.3 1.8 copy-start.29
  12.7 1.0 copy-start.16
  13.7 3.7 copy-start.26
  17.3 52.1 %all-to-all-start = ((bf16[2,1,4,256,384]{4,0,2,1,3:T(2,128)(2,1)}), bf16[2,1,4,256,384]{4,0,2,1,3:T(2,128)(2,1)}, u32[]{:S(2)}, u32[]{:S(2)}) async-start(bf16[2,1,4,256,384]{4,0,2,1,3:T(2,128)(2,1)} %copy.59), calls=%async_computation | async-start | bytes 3145728 | tf_op jit(solution)/shard_map/all_to_all | solution.py:85
  34.6 40.6 %copy-start.3 = (bf16[1,256,4,384]{1,3,2,0:T(8,128)(2,1)}, bf16[1,256,4,384]{1,3,2,0:T(8,128)(2,1)S(1)}, u32[]{:S(2)}) copy-start(bf16[1,256,4,384]{1,3,2,0:T(8,128)(2,1)S(1)} %copy.111) | copy-start | bytes 2359300
  36.5 38.8 %copy-start.5 = (bf16[1,256,4,384]{1,3,2,0:T(8,128)(2,1)}, bf16[1,256,4,384]{1,3,2,0:T(8,128)(2,1)S(1)}, u32[]{:S(2)}) copy-start(bf16[1,256,4,384]{1,3,2,0:T(8,128)(2,1)S(1)} %copy.113) | copy-start | bytes 2359300
  71.5 1.0 copy-start.12
  75.2 1.0 copy-start.23
  133.8 15.6 %copy-start.20 = (bf16[1,4,256,384]{3,2,1,0:T(8,128)(2,1)}, bf16[1,4,256,384]{3,2,1,0:T(8,128)(2,1)S(1)}, u32[]{:S(2)}) copy-start(bf16[1,4,256,384]{3,2,1,0:T(8,128)(2,1)S(1)} %multiply_convert_fusion.4) | copy-start | bytes 2359300
  133.9 15.5 %copy-start.18 = (bf16[1,4,256,384]{3,2,1,0:T(8,128)(2,1)S(1)}, bf16[1,4,256,384]{3,2,1,0:T(8,128)(2,1)}, u32[]{:S(2)}) copy-start(bf16[1,4,256,384]{3,2,1,0:T(8,128)(2,1)} %param.8) | copy-start | bytes 2359300
  133.9 15.5 %copy-start.31 = (bf16[1536,384]{1,0:T(8,128)(2,1)S(1)}, bf16[1536,384]{1,0:T(8,128)(2,1)}, u32[]{:S(2)}) copy-start(bf16[1536,384]{1,0:T(8,128)(2,1)} %param.11) | copy-start | bytes 3538948
  152.7 1.9 copy-start.32
  154.6 1.2 copy-start.1
  167.1 47.5 %all-to-all-start.2 = ((bf16[2,1,4,256,384]{4,0,2,1,3:T(2,128)(2,1)}), bf16[2,1,4,256,384]{4,0,2,1,3:T(2,128)(2,1)S(1)}, u32[]{:S(2)}, u32[]{:S(2)}) async-start(bf16[2,1,4,256,384]{4,0,2,1,3:T(2,128)(2,1)} %copy.74), calls=%async_computation.2 | async-start | bytes 3145728 | tf_op jit(solution)/shard_map/all_to_all | solution.py:85
  174.7 328.6 %all-reduce.4.cloned.1.call-start = ((), (), s32[]{:S(2)}) async-start(), calls=%async_computation.5 | async-start | bytes 9437184 | tf_op jit(solution)/shard_map/psum | solution.py:133
  175.0 5.1 copy-start.19
  175.0 5.1 copy-start.33
  183.4 409.4 %all-gather.2.cloned.1.call-start = ((), (), s32[]{:S(2)}) async-start(), calls=%async_computation.4 | async-start | bytes 7864320 | tf_op jit(solution)/shard_map/all_gather | solution.py:12
  215.2 1.0 copy-start.11
  215.2 1.0 copy-start.13
  216.3 2.2 copy-start.2
  220.3 1.1 copy-start.4
  220.3 1.4 copy-start.6
  221.7 2.1 copy-start.22
  221.7 2.1 copy-start.24
  227.9 279.7 %all-to-all-start.3 = ((bf16[2,1,256,4,384]{4,0,3,1,2:T(2,128)(2,1)}), bf16[2,1,256,4,384]{4,0,3,1,2:T(2,128)(2,1)S(1)}, u32[]{:S(2)}, u32[]{:S(2)}) async-start(bf16[2,1,256,4,384]{4,0,3,1,2:T(2,128)(2,1)} %copy.80), calls=%async_computation.3 | async-start | bytes 3145728 | tf_op jit(solution)/shard_map/all_to_all | solution.py:94
  503.3 3.0 copy-start.9
  508.1 1.0 copy-start.17
  509.1 1.4 copy-start.7
  509.1 1.6 copy-start.8
  511.5 2.3 copy-start.28
  (7 other events, 6.3 us)
Sparse Core Ops, SparseCore 0:
  183.5 319.7 all-reduce.3
Sparse Core Ops, SparseCore 1:
  220.4 70.0 all-gather.1
